TPU v7x, 32 devices: a whole 2x2x4 slice. The times are simulated.
32 devices in a mesh: dp: 4 (over y, core), row: 4 (over z), col: 2 (over x).
Axes of the slice: x: 2, y: 2, z: 4, core: 2. Of those that a mesh axis runs over, the one named last changes fastest.
Arguments:
- inputs: bfloat16 [4096, 1024], P(('dp', 'col'), 'row'), may hold values from -6 to 6
- cotangent: bfloat16 [4096, 1024], P(('dp', 'col'), 'row'), may hold values from -6 to 6
- seg_parent: int32 [52], P('dp'), may hold values from 0 to 51, as said below
- token_depth: int32 [4096], P('dp'), may hold values from 0 to 383, as said below
- ln1_gain: float32 [1024], P('row'), may hold values from 0.25 to 1.75
- ln1_bias: float32 [1024], P('row'), may hold values from -1.5 to 1.5
- w_qkv: bfloat16 [1024, 3, 1024], P('row', None, 'col'), may hold values from -0.1875 to 0.1875
- b_qv: float32 [2, 1024], P(None, 'col'), may hold values from -1.5 to 1.5
- w_out: bfloat16 [1024, 1024], P('col', 'row'), may hold values from -0.5 to 0.5
- b_out: float32 [1024], P('row'), may hold values from -1.5 to 1.5
- ln2_gain: float32 [1024], P('row'), may hold values from 0.25 to 1.75
- ln2_bias: float32 [1024], P('row'), may hold values from -1.5 to 1.5
- w_up: bfloat16 [1024, 4096], P('row', 'col'), may hold values from -0.1875 to 0.1875
- b_up: float32 [4096], P('col'), may hold values from -1.5 to 1.5
- w_down: bfloat16 [4096, 1024], P('col', 'row'), may hold values from -0.125 to 0.125
- b_down: float32 [1024], P('row'), may hold values from -1.5 to 1.5
Outputs:
- result: float32 [4096, 1024], P(('dp', 'col'), 'row')
- input_grad: float32 [4096, 1024], P(('dp', 'col'), 'row')
- grad_ln1_gain: float32 [1024], P('row')
- grad_ln1_bias: float32 [1024], P('row')
- grad_w_qkv: float32 [1024, 3, 1024], P('row', None, 'col')
- grad_b_qv: float32 [2, 1024], P(None, 'col')
- grad_w_out: float32 [1024, 1024], P('col', 'row')
- grad_b_out: float32 [1024], P('row')
- grad_ln2_gain: float32 [1024], P('row')
- grad_ln2_bias: float32 [1024], P('row')
- grad_w_up: float32 [1024, 4096], P('row', 'col')
- grad_b_up: float32 [4096], P('col')
- grad_w_down: float32 [4096, 1024], P('col', 'row')
- grad_b_down: float32 [1024], P('row')
Inputs may be any that keep to these rules, and one draw needn't show every extreme that they name: `seg_parent`: tree t holds tokens t * 1024 to (t + 1) * 1024 - 1 and segments 13 t to 13 t + 12, laid out as segment(i) says: segment 13 t is the trunk of 256 tokens and is its own parent; four of the other twelve are branches with the trunk as parent, eight are leaves, two for every branch, with that branch as parent; segment 13 t + 12 is a branch; which ids play the other parts is drawn. `token_depth`: the token at offset j of its segment has depth j in a trunk, 256 + j in a branch and 320 + j in a leaf.
All inputs are finite; a program needn't handle non-finite values.
Results may differ from a plain program's by a relative error of at most 0.011.
Values may be sent and summed in bfloat16 or wider, within the bound.
A program may use at most 192 MiB of HBM per device.

v0:
```python
import math
import jax
import jax.numpy as jnp
from jax import lax
from jax.sharding import PartitionSpec as P

HD = 128
EPS = 1e-05
MASKED = -1e30


def gelu_value(values):
    return 0.5 * values * (1.0 + jax.scipy.special.erf(values / math.sqrt(2.0)))


def gelu_slope(values):
    return 0.5 * (1.0 + jax.scipy.special.erf(values / math.sqrt(2.0))) + values * jnp.exp(
        -0.5 * values * values
    ) / math.sqrt(2.0 * math.pi)


def width_sums(first_term, second_term):
    return lax.psum((jnp.sum(first_term, axis=1), jnp.sum(second_term, axis=1)), "row")


def normalize(values, norm_gain, norm_bias, feature_count):
    row_total, square = width_sums(values, values * values)
    row_mean = row_total / feature_count
    inv_std = lax.rsqrt(square / feature_count - row_mean * row_mean + EPS)
    normed = (values - row_mean[:, None]) * inv_std[:, None]
    return (normed, inv_std, (normed * norm_gain + norm_bias).astype(jnp.bfloat16))


def normalize_back(upstream, normed, inv_std, norm_gain, feature_count):
    spread = upstream * norm_gain
    row_total, cross_sum = width_sums(spread, spread * normed)
    return inv_std[:, None] * (
        spread - row_total[:, None] / feature_count - normed * (cross_sum[:, None] / feature_count)
    )


def contract(left_op, right_op, flipped):
    if flipped:
        return lax.dot_general(
            left_op, right_op, (((1,), (1,)), ((), ())), preferred_element_type=jnp.float32
        )
    return jnp.dot(left_op, right_op, preferred_element_type=jnp.float32)


def outer_sum(left_op, right_op):
    return lax.dot_general(
        left_op, right_op, (((0,), (0,)), ((), ())), preferred_element_type=jnp.float32
    )


def across_rows(operand, weight_block, flipped):
    gathered = lax.all_gather(operand, "col", axis=0, tiled=True)
    row_count = gathered.shape[0] // lax.axis_size("row")

    def partial_term(row_start, row_num):
        return contract(gathered, weight_block, flipped)

    return (
        lax.psum_scatter(
            partial_term(jnp.int32(0), row_count * lax.axis_size("row")),
            "row",
            scatter_dimension=0,
            tiled=True,
        ),
        gathered,
    )


def across_cols(operand, weight_block, flipped):
    gathered = lax.all_gather(operand, "row", axis=0, tiled=True)
    row_count = gathered.shape[0] // lax.axis_size("col")

    def partial_term(row_start, row_num):
        return contract(gathered, weight_block, flipped)

    return (
        lax.psum_scatter(
            partial_term(jnp.int32(0), row_count * lax.axis_size("col")),
            "col",
            scatter_dimension=0,
            tiled=True,
        ),
        gathered,
    )


def tree_labels(seg_parent, token_depth):
    seg_count = seg_parent.shape[0]
    tree_len = token_depth.shape[0]
    seg_len = tree_len // 16
    slot_ids = jnp.arange(seg_count, dtype=jnp.int32)
    where_at = jnp.arange(tree_len, dtype=jnp.int32)
    segment = jnp.where(where_at < 4 * seg_len, 0, 1 + (where_at - 4 * seg_len) // seg_len)
    parent_local = seg_parent - lax.axis_index("dp") * seg_count
    parent_one = jnp.sum(
        jnp.where(segment[:, None] == slot_ids[None, :], parent_local[None, :], 0), axis=1
    )
    parent_two = jnp.sum(
        jnp.where(parent_one[:, None] == slot_ids[None, :], parent_local[None, :], 0), axis=1
    )
    return (segment, parent_one, parent_two, token_depth)


def block_scores(query_block, key_rows, labels, query_start, slopes):
    segment, parent_one, parent_two, token_depth = labels
    block_size = query_block.shape[0]
    query_seg = lax.dynamic_slice_in_dim(segment, query_start, block_size, 0)
    query_one = lax.dynamic_slice_in_dim(parent_one, query_start, block_size, 0)
    query_two = lax.dynamic_slice_in_dim(parent_two, query_start, block_size, 0)
    query_depth = lax.dynamic_slice_in_dim(token_depth, query_start, block_size, 0)
    allowed = (
        (segment[None, :] == query_seg[:, None])
        | (segment[None, :] == query_one[:, None])
        | (segment[None, :] == query_two[:, None])
    ) & (token_depth[None, :] <= query_depth[:, None])
    score_scale = query_block.shape[2] ** (-0.5)
    raw = jnp.einsum("qhd,khd->hqk", query_block, key_rows, preferred_element_type=jnp.float32)
    distance = (query_depth[:, None] - token_depth[None, :]).astype(jnp.float32)
    scores = raw * score_scale - slopes[:, None, None] * distance[None]
    return jnp.where(allowed[None], scores, MASKED)


def attention_forward(queries, key_rows, value_rows, labels, slopes, offset):
    block_size = min(512, queries.shape[0])
    blocks = queries.shape[0] // block_size

    def one_block(block_index):
        block_first = block_index * block_size
        query_block = lax.dynamic_slice_in_dim(queries, block_first, block_size, 0)
        scores = block_scores(query_block, key_rows, labels, offset + block_first, slopes)
        top_score = jnp.max(scores, axis=2, keepdims=True)
        weights = jnp.exp(scores - top_score)
        weight_total = jnp.sum(weights, axis=2, keepdims=True)
        probs = (weights / weight_total).astype(jnp.bfloat16)
        mixed = jnp.einsum("hqk,khd->qhd", probs, value_rows, preferred_element_type=jnp.float32)
        return (mixed, (top_score + jnp.log(weight_total))[:, :, 0])

    return lax.map(one_block, jnp.arange(blocks, dtype=jnp.int32))


def attention_backward(
    queries, key_rows, value_rows, grad_mixed, log_total, labels, slopes, offset
):
    block_size = min(512, queries.shape[0])
    blocks = queries.shape[0] // block_size
    score_scale = queries.shape[2] ** (-0.5)

    def one_block(carry, items):
        key_grad, value_grad = carry
        block_index, block_total = items
        block_first = block_index * block_size
        query_block = lax.dynamic_slice_in_dim(queries, block_first, block_size, 0)
        grad_block = lax.dynamic_slice_in_dim(grad_mixed, block_first, block_size, 0)
        scores = block_scores(query_block, key_rows, labels, offset + block_first, slopes)
        probs = jnp.exp(scores - block_total[:, :, None])
        grad_probs = jnp.einsum(
            "qhd,khd->hqk", grad_block, value_rows, preferred_element_type=jnp.float32
        )
        centre = jnp.sum(probs * grad_probs, axis=2, keepdims=True)
        grad_scores = (probs * (grad_probs - centre)).astype(jnp.bfloat16)
        query_grad = (
            jnp.einsum("hqk,khd->qhd", grad_scores, key_rows, preferred_element_type=jnp.float32)
            * score_scale
        )
        key_grad = (
            key_grad
            + jnp.einsum(
                "hqk,qhd->khd", grad_scores, query_block, preferred_element_type=jnp.float32
            )
            * score_scale
        )
        value_grad = value_grad + jnp.einsum(
            "hqk,qhd->khd",
            probs.astype(jnp.bfloat16),
            grad_block,
            preferred_element_type=jnp.float32,
        )
        return ((key_grad, value_grad), query_grad)

    empty = jnp.zeros(key_rows.shape, jnp.float32)
    (key_grad, value_grad), query_grad = lax.scan(
        one_block, (empty, empty), (jnp.arange(blocks, dtype=jnp.int32), log_total)
    )
    return (key_grad, value_grad, query_grad)


def on_device(
    inputs,
    cotangent,
    seg_parent,
    token_depth,
    ln1_gain,
    ln1_bias,
    w_qkv,
    b_qv,
    w_out,
    b_out,
    ln2_gain,
    ln2_bias,
    w_up,
    b_up,
    w_down,
    b_down,
):
    feature_count = inputs.shape[1] * lax.axis_size("row")
    col_width = w_qkv.shape[2]
    heads_here = col_width // HD
    qkv_flat = w_qkv.reshape(w_qkv.shape[0], 3 * col_width)
    labels = tree_labels(seg_parent, token_depth)
    heads_seen = lax.axis_index("col") * heads_here + jnp.arange(heads_here, dtype=jnp.int32)
    slopes = jnp.exp2(-(heads_seen + 1).astype(jnp.float32))
    states = inputs.astype(jnp.float32)
    normed_one, inv_one, entry_one = normalize(states, ln1_gain, ln1_bias, feature_count)
    projected, entry_one_all = across_rows(entry_one, qkv_flat, False)
    tok_rows = projected.shape[0]
    projected = projected.reshape(tok_rows, 3, col_width)
    queries = (projected[:, 0] + b_qv[0]).astype(jnp.bfloat16)
    keys_here = projected[:, 1].astype(jnp.bfloat16)
    values_here = (projected[:, 2] + b_qv[1]).astype(jnp.bfloat16)
    pair_all = lax.all_gather(
        jnp.stack([keys_here, values_here], axis=1), "row", axis=0, tiled=True
    )
    key_rows = pair_all[:, 0].reshape(-1, heads_here, HD)
    value_rows = pair_all[:, 1].reshape(-1, heads_here, HD)
    query_heads = queries.reshape(tok_rows, heads_here, HD)
    offset = lax.axis_index("row") * tok_rows
    mixed, log_total = attention_forward(query_heads, key_rows, value_rows, labels, slopes, offset)
    mixed = mixed.reshape(tok_rows, col_width).astype(jnp.bfloat16)
    attn_out, mixed_all = across_cols(mixed, w_out, False)
    middle = states + attn_out + b_out
    normed_two, inv_two, entry_two = normalize(middle, ln2_gain, ln2_bias, feature_count)
    hidden_pre, entry_two_all = across_rows(entry_two, w_up, False)
    hidden_pre = hidden_pre + b_up
    hidden = gelu_value(hidden_pre).astype(jnp.bfloat16)
    ffn_out, hidden_all = across_cols(hidden, w_down, False)
    result = middle + ffn_out + b_down
    grad_hidden, down_all = across_rows(cotangent, w_down, True)
    grad_pre = (grad_hidden * gelu_slope(hidden_pre)).astype(jnp.bfloat16)
    grad_entry_two, pre_all = across_cols(grad_pre, w_up, True)
    grad_middle = cotangent.astype(jnp.float32) + normalize_back(
        grad_entry_two, normed_two, inv_two, ln2_gain, feature_count
    )
    grad_branch = grad_middle.astype(jnp.bfloat16)
    grad_mixed, branch_all = across_rows(grad_branch, w_out, True)
    grad_mixed = grad_mixed.astype(jnp.bfloat16).reshape(tok_rows, heads_here, HD)
    key_grad, value_grad, query_grad = attention_backward(
        query_heads, key_rows, value_rows, grad_mixed, log_total, labels, slopes, offset
    )
    kv_grads = lax.psum_scatter(
        jnp.stack([key_grad.reshape(-1, col_width), value_grad.reshape(-1, col_width)], axis=1),
        "row",
        scatter_dimension=0,
        tiled=True,
    )
    grad_projected = jnp.stack(
        [
            query_grad.reshape(tok_rows, col_width).astype(jnp.bfloat16),
            kv_grads[:, 0].astype(jnp.bfloat16),
            kv_grads[:, 1].astype(jnp.bfloat16),
        ],
        axis=1,
    )
    grad_entry_one, proj_all = across_cols(
        grad_projected.reshape(tok_rows, 3 * col_width), qkv_flat, True
    )
    input_grad = grad_middle + normalize_back(
        grad_entry_one, normed_one, inv_one, ln1_gain, feature_count
    )
    proj_sums = jnp.sum(proj_all.astype(jnp.float32), axis=0).reshape(3, col_width)
    weight_terms = (
        outer_sum(entry_one_all, proj_all).reshape(w_qkv.shape),
        jnp.stack([proj_sums[0], proj_sums[2]], axis=0),
        outer_sum(mixed_all, branch_all),
        jnp.sum(branch_all.astype(jnp.float32), axis=0),
        outer_sum(entry_two_all, pre_all),
        jnp.sum(pre_all.astype(jnp.float32), axis=0),
        outer_sum(hidden_all, down_all),
        jnp.sum(down_all.astype(jnp.float32), axis=0),
    )
    (
        grad_w_qkv,
        grad_b_qv,
        grad_w_out,
        grad_b_out,
        grad_w_up,
        grad_b_up,
        grad_w_down,
        grad_b_down,
    ) = lax.psum(
        (
            weight_terms[0],
            weight_terms[1],
            weight_terms[2],
            weight_terms[3],
            weight_terms[4],
            weight_terms[5],
            weight_terms[6],
            weight_terms[7],
        ),
        "dp",
    )
    norm_terms = (
        jnp.sum(grad_entry_one * normed_one, axis=0),
        jnp.sum(grad_entry_one, axis=0),
        jnp.sum(grad_entry_two * normed_two, axis=0),
        jnp.sum(grad_entry_two, axis=0),
    )
    grad_ln1_gain, grad_ln1_bias, grad_ln2_gain, grad_ln2_bias = lax.psum(
        (norm_terms[0], norm_terms[1], norm_terms[2], norm_terms[3]), ("dp", "col")
    )
    return (
        result,
        input_grad,
        grad_ln1_gain,
        grad_ln1_bias,
        grad_w_qkv,
        grad_b_qv,
        grad_w_out,
        grad_b_out,
        grad_ln2_gain,
        grad_ln2_bias,
        grad_w_up,
        grad_b_up,
        grad_w_down,
        grad_b_down,
    )


def solution(mesh):
    placed = (
        P(("dp", "col"), "row"),
        P(("dp", "col"), "row"),
        P("dp"),
        P("dp"),
        P("row"),
        P("row"),
        P("row", None, "col"),
        P(None, "col"),
        P("col", "row"),
        P("row"),
        P("row"),
        P("row"),
        P("row", "col"),
        P("col"),
        P("col", "row"),
        P("row"),
    )
    return jax.shard_map(
        on_device,
        mesh=mesh,
        in_specs=placed,
        out_specs=(
            P(("dp", "col"), "row"),
            P(("dp", "col"), "row"),
            P("row"),
            P("row"),
            P("row", None, "col"),
            P(None, "col"),
            P("col", "row"),
            P("row"),
            P("row"),
            P("row"),
            P("row", "col"),
            P("col"),
            P("col", "row"),
            P("row"),
        ),
        check_vma=False,
    )
```

profile of v0, /device:TPU:0, one launch (start us, length us, event | category | flops | bytes accessed | tf_op | source)
XLA Modules:
  0.0 1127.7 jit_solution(2528115706905828047)
XLA Ops:
  8.5 13.5 %all-reduce.4 = (f32[512]{0:T(512)S(1)}, f32[512]{0:T(512)S(1)}) all-reduce(f32[512]{0:T(512)S(1)} %get-tuple-element.134, f32[512]{0:T(512)S(1)} %get-tuple-element.133), channel_id=1, replica_groups=mesh['dp'=4,'row'=4,'col'=2] {'row'}, use_global_device_ids=true, to_apply=%region_3.4 | all-reduce | flops 1024 | bytes 8192 | tf_op jit(solution)/shard_map/psum | solution.py:23
  23.1 7.0 all_gather.27
  31.8 3.7 fusion.46
  36.2 108.4 %reduce-scatter.10.cloned.1.call-done = f32[256,1536]{1,0:T(8,128)} async-done(((f32[1024,1536]{1,0:T(8,128)}), f32[256,1536]{1,0:T(8,128)}) %reduce-scatter.10.cloned.1.call-update) | async-done | bytes 1572880 | tf_op jit(solution)/shard_map/reduce_scatter | solution.py:64
  144.6 1.9 copy.48
  149.7 44.8 %all-gather.6.cloned.1.call-done = bf16[1024,2,512]{0,2,1:T(8,128)(2,1)} async-done(((bf16[256,2,512]{0,2,1:T(8,128)(2,1)}), bf16[1024,2,512]{0,2,1:T(8,128)(2,1)}) %all-gather.6.cloned.1.call-update) | async-done | bytes 2097168 | tf_op jit(solution)/shard_map/all_gather | solution.py:225
  194.5 1.8 fusion.41
  196.4 1.8 fusion.45
  199.2 1.9 fusion.13
  201.1 28.5 %all-gather.8.cloned.1.call-done = bf16[1024,512]{0,1:T(8,128)(2,1)} async-done(((bf16[256,512]{0,1:T(8,128)(2,1)}), bf16[1024,512]{0,1:T(8,128)(2,1)}) %all-gather.8.cloned.1.call-update) | async-done | bytes 1048592 | tf_op jit(solution)/shard_map/all_gather | solution.py:75
  229.7 2.7 fusion.47
  232.4 10.4 all_gather.32
  243.6 5.8 fusion.50
  249.5 2.9 reduce-scatter.12.cloned.1.call-done
  253.7 10.6 all-reduce.3
  264.5 7.0 all_gather.30
  272.3 4.5 fusion.48
  276.9 121.6 %reduce-scatter.18.cloned.1.call-done = f32[256,2048]{1,0:T(8,128)} async-done(((f32[1024,2048]{1,0:T(8,128)}), f32[256,2048]{1,0:T(8,128)}) %reduce-scatter.18.cloned.1.call-update) | async-done | bytes 2097168 | tf_op jit(solution)/shard_map/reduce_scatter | solution.py:64
  398.5 147.5 %reduce-scatter.14.cloned.1.call-done = f32[256,2048]{1,0:T(8,128)} async-done(((f32[1024,2048]{1,0:T(8,128)}), f32[256,2048]{1,0:T(8,128)}) %reduce-scatter.14.cloned.1.call-update) | async-done | bytes 2097168 | tf_op jit(solution)/shard_map/reduce_scatter | solution.py:64
  546.0 3.7 fusion.7
  550.7 80.7 %all-gather.12.cloned.1.call-done = bf16[1024,2048]{1,0:T(8,128)(2,1)} async-done(((bf16[256,2048]{1,0:T(8,128)(2,1)}), bf16[1024,2048]{1,0:T(8,128)(2,1)}) %all-gather.12.cloned.1.call-update) | async-done | bytes 4194320 | tf_op jit(solution)/shard_map/all_gather | solution.py:75
  631.3 4.4 fusion.51
  635.9 77.0 %all-gather.10.cloned.1.call-done = bf16[1024,2048]{1,0:T(8,128)(2,1)} async-done(((bf16[256,2048]{1,0:T(8,128)(2,1)}), bf16[1024,2048]{1,0:T(8,128)(2,1)}) %all-gather.10.cloned.1.call-update) | async-done | bytes 4194320 | tf_op jit(solution)/shard_map/all_gather | solution.py:75
  712.9 4.7 fusion.49
  717.7 17.0 %reduce-scatter.20.cloned.1.call-done = f32[512,256]{1,0:T(8,128)} async-done(((f32[1024,256]{1,0:T(8,128)}), f32[512,256]{1,0:T(8,128)}) %reduce-scatter.20.cloned.1.call-update) | async-done | bytes 524304 | tf_op jit(solution)/shard_map/reduce_scatter | solution.py:82
  736.1 11.7 %all-reduce.2 = (f32[512]{0:T(512)S(1)}, f32[512]{0:T(512)S(1)}) all-reduce(f32[512]{0:T(512)S(1)} %get-tuple-element.124, f32[512]{0:T(512)S(1)} %get-tuple-element.128), channel_id=1, replica_groups=mesh['dp'=4,'row'=4,'col'=2] {'row'}, use_global_device_ids=true, to_apply=%region_21.22 | all-reduce | flops 1024 | bytes 8192 | tf_op jit(solution)/shard_map/psum | solution.py:23
  747.8 9.9 reduce-scatter.16.cloned.1.call-done
  757.7 2.4 fusion.39
  760.1 8.7 all_gather.34
  768.8 1.8 fusion.52
  770.7 44.0 %reduce-scatter.22.cloned.1.call-done = f32[256,512]{1,0:T(8,128)} async-done(((f32[1024,512]{1,0:T(8,128)}), f32[256,512]{1,0:T(8,128)}) %reduce-scatter.22.cloned.1.call-update) | async-done | bytes 524304 | tf_op jit(solution)/shard_map/reduce_scatter | solution.py:64
  815.8 3.3 fusion.8
  822.1 2.4 pad_maximum_fusion
  824.6 2.8 fusion.12
  827.4 73.4 %reduce-scatter.24.cloned.1.call-done = f32[256,2,512]{0,2,1:T(8,128)} async-done(((f32[1024,2,512]{0,2,1:T(8,128)}), f32[256,2,512]{0,2,1:T(8,128)}) %reduce-scatter.24.cloned.1.call-update) | async-done | bytes 1048592 | tf_op jit(solution)/shard_map/reduce_scatter | solution.py:254
  902.1 1.9 pad_maximum_fusion.1
  904.1 64.0 %all-gather.14.cloned.1.call-done = bf16[1024,1536]{0,1:T(8,128)(2,1)} async-done(((bf16[256,1536]{0,1:T(8,128)(2,1)}), bf16[1024,1536]{0,1:T(8,128)(2,1)}) %all-gather.14.cloned.1.call-update) | async-done | bytes 3145744 | tf_op jit(solution)/shard_map/all_gather | solution.py:75
  968.1 3.9 fusion.53
  972.3 4.9 fusion.55
  977.3 2.7 fusion.56
  981.2 2.1 fusion.57
  983.6 3.0 convert_reduce_fusion
  987.3 11.7 %all-reduce.5 = (f32[2,512]{1,0:T(2,128)}, f32[256]{0:T(256)}, f32[2048]{0:T(1024)}, f32[256]{0:T(256)}) all-reduce(f32[2,512]{1,0:T(2,128)S(1)} %pad_maximum_fusion.3, f32[256]{0:T(256)S(1)} %convert_reduce_fusion.3, f32[2048]{0:T(1024)S(1)} %convert_reduce_fusion, ...), channel_id=1, replica_groups=mesh['dp'=4,'row'=4,'col'=2] {'dp'}, use_global_device_ids=true, to_apply=%region_36.37 | all-reduce | flops 3584 | bytes 28672 | tf_op jit(solution)/shard_map/psum | solution.py:294
  1000.6 14.2 %all-reduce = (f32[256]{0:T(256)}, f32[256]{0:T(256)}, f32[256]{0:T(256)}, f32[256]{0:T(256)}) all-reduce(f32[256]{0:T(256)S(1)} %get-tuple-element.125, f32[256]{0:T(256)S(1)} %get-tuple-element.130, f32[256]{0:T(256)S(1)} %get-tuple-element.123, f32[256]{0:T(256)S(1)} %get-tuple-element.129), channel_id=1, replica_groups=mesh['dp'=4,'row'=4,'col'=2] {'dp','col'}, use_global_device_ids=true, to_apply=%region_31.32 | all-reduce | flops 1024 | bytes 8192 | tf_op jit(solution)/shard_map/psum | solution.py:313
  1014.8 8.9 all-reduce.1
  1023.7 2.2 fusion.24
  1025.9 88.7 %all-reduce.9.cloned.1.call-done = (f32[256,3,512]{0,2,1:T(8,128)}, f32[512,256]{1,0:T(8,128)}, f32[256,2048]{1,0:T(8,128)}, f32[2048,256]{1,0:T(8,128)}) async-done(((f32[256,3,512]{0,2,1:T(8,128)}, f32[512,256]{1,0:T(8,128)}, f32[256,2048]{1,0:T(8,128)}, f32[2048,256]{1,0:T(8,128)}), (f32[256,3,512]{0,2,1:T(8,128)}, f32[512,256]{1,0:T(8,128)}, f32[256,2048]{1,0:T(8,128)}, ...) | async-done | bytes 6291472 | tf_op jit(solution)/shard_map/psum | solution.py:294
  1114.6 3.2 copy.55
  (147 shorter events, 27.9 us)
Async XLA Ops:
  7.2 265.1 %copy-start = (bf16[256,2048]{1,0:T(8,128)(2,1)S(1)}, bf16[256,2048]{1,0:T(8,128)(2,1)}, u32[]{:S(2)}) copy-start(bf16[256,2048]{1,0:T(8,128)(2,1)} %param.28) | copy-start | bytes 3145732
  7.2 137.4 %reduce-scatter.10.cloned.1.call-start = ((), (), s32[]{:S(2)}) async-start(), calls=%async_computation.9 | async-start | bytes 7864320 | tf_op jit(solution)/shard_map/reduce_scatter | solution.py:64
  30.2 5.3 copy-start.9
  31.8 3.7 copy-start.13
  35.5 159.0 %all-gather.6.cloned.1.call-start = ((), (), s32[]{:S(2)}) async-start(), calls=%async_computation.10 | async-start | bytes 2621440 | tf_op jit(solution)/shard_map/all_gather | solution.py:225
  36.2 111.5 %copy-start.26 = (s32[1024]{0:T(1024)S(1)}, s32[1024]{0:T(1024)}, u32[]{:S(2)}) copy-start(s32[1024]{0:T(1024)} %param.19) | copy-start | bytes 12292
  36.2 111.7 %copy-start.35 = (s32[13]{0:T(128)S(1)}, s32[13]{0:T(128)}, u32[]{:S(2)}) copy-start(s32[13]{0:T(128)} %param.18) | copy-start | bytes 160
  146.7 49.7 %copy-start.19 = (f32[256,1,512]{0,2,1:T(8,128)}, f32[256,1,512]{0,2,1:T(8,128)S(1)}, u32[]{:S(2)}) copy-start(f32[256,1,512]{0,2,1:T(8,128)S(1)} %get-tuple-element.162) | copy-start | bytes 1572868
  147.6 82.1 %all-gather.8.cloned.1.call-start = ((), (), s32[]{:S(2)}) async-start(), calls=%async_computation.11 | async-start | bytes 1310720 | tf_op jit(solution)/shard_map/all_gather | solution.py:75
  194.5 1.9 copy-start.22
  196.3 1.8 copy-start.8
  198.1 2.9 copy-start.2
  199.2 30.5 %copy-start.24 = (bf16[512,256]{1,0:T(8,128)(2,1)S(1)}, bf16[512,256]{1,0:T(8,128)(2,1)}, u32[]{:S(2)}) copy-start(bf16[512,256]{1,0:T(8,128)(2,1)} %param.24) | copy-start | bytes 786436
  201.1 31.4 %copy-start.23 = (bf16[512,256]{1,0:T(8,128)(2,1)S(1)}, bf16[512,256]{1,0:T(8,128)(2,1)}, u32[]{:S(2)}) copy-start(bf16[512,256]{1,0:T(8,128)(2,1)} %param.17) | copy-start | bytes 786436
  201.1 51.3 %reduce-scatter.12.cloned.1.call-start = ((), (), s32[]{:S(2)}) async-start(), calls=%async_computation.12 | async-start | bytes 1572864 | tf_op jit(solution)/shard_map/reduce_scatter | solution.py:82
  232.4 166.1 %reduce-scatter.18.cloned.1.call-start = ((), (), s32[]{:S(2)}) async-start(), calls=%async_computation.16 | async-start | bytes 10485760 | tf_op jit(solution)/shard_map/reduce_scatter | solution.py:64
  249.4 3.0 copy-start.4
  249.4 3.0 copy-start.33
  249.4 14.9 %copy-start.27 = (f32[256]{0:T(256)S(1)}, f32[256]{0:T(256)}, u32[]{:S(2)}) copy-start(f32[256]{0:T(256)} %param.26) | copy-start | bytes 3076
  249.4 14.9 %copy-start.31 = (f32[256]{0:T(256)S(1)}, f32[256]{0:T(256)}, u32[]{:S(2)}) copy-start(f32[256]{0:T(256)} %param.27) | copy-start | bytes 3076
  249.4 296.6 %reduce-scatter.14.cloned.1.call-start = ((), (), s32[]{:S(2)}) async-start(), calls=%async_computation.13 | async-start | bytes 10485760 | tf_op jit(solution)/shard_map/reduce_scatter | solution.py:64
  276.8 269.2 %copy-start.29 = (f32[2048]{0:T(1024)S(1)}, f32[2048]{0:T(1024)}, u32[]{:S(2)}) copy-start(f32[2048]{0:T(1024)} %param.29) | copy-start | bytes 24580
  276.8 354.5 %all-gather.12.cloned.1.call-start = ((), (), s32[]{:S(2)}) async-start(), calls=%async_computation.17 | async-start | bytes 5242880 | tf_op jit(solution)/shard_map/all_gather | solution.py:75
  549.7 163.2 %all-gather.10.cloned.1.call-start = ((), (), s32[]{:S(2)}) async-start(), calls=%async_computation.14 | async-start | bytes 5242880 | tf_op jit(solution)/shard_map/all_gather | solution.py:75
  550.5 184.2 %reduce-scatter.20.cloned.1.call-start = ((), (), s32[]{:S(2)}) async-start(), calls=%async_computation.18 | async-start | bytes 1572864 | tf_op jit(solution)/shard_map/reduce_scatter | solution.py:82
  635.8 121.9 %copy-start.32 = (f32[256]{0:T(256)S(1)}, f32[256]{0:T(256)}, u32[]{:S(2)}) copy-start(f32[256]{0:T(256)} %param.31) | copy-start | bytes 3076
  635.8 121.9 %reduce-scatter.16.cloned.1.call-start = ((), (), s32[]{:S(2)}) async-start(), calls=%async_computation.15 | async-start | bytes 1572864 | tf_op jit(solution)/shard_map/reduce_scatter | solution.py:82
  717.6 97.0 %reduce-scatter.22.cloned.1.call-start = ((), (), s32[]{:S(2)}) async-start(), calls=%async_computation.19 | async-start | bytes 2621440 | tf_op jit(solution)/shard_map/reduce_scatter | solution.py:64
  770.6 130.2 %reduce-scatter.24.cloned.1.call-start = ((), (), s32[]{:S(2)}) async-start(), calls=%async_computation.20 | async-start | bytes 5242880 | tf_op jit(solution)/shard_map/reduce_scatter | solution.py:254
  815.8 3.5 copy-start.3
  820.6 1.0 copy-start.20
  824.6 143.5 %all-gather.14.cloned.1.call-start = ((), (), s32[]{:S(2)}) async-start(), calls=%async_computation.21 | async-start | bytes 3932160 | tf_op jit(solution)/shard_map/all_gather | solution.py:75
  827.4 140.7 %copy-start.14 = (bf16[256,3,512]{0,2,1:T(8,128)(2,1)S(1)}, bf16[256,3,512]{0,2,1:T(8,128)(2,1)}, u32[]{:S(2)}) copy-start(bf16[256,3,512]{0,2,1:T(8,128)(2,1)} %copy-done.13) | copy-start | bytes 2359300
  904.0 68.3 %copy-start.16 = (bf16[1024,256]{1,0:T(8,128)(2,1)S(1)}, bf16[1024,256]{1,0:T(8,128)(2,1)}, u32[]{:S(2)}) copy-start(bf16[1024,256]{1,0:T(8,128)(2,1)} %copy-done.15) | copy-start | bytes 1572868
  904.0 95.0 %reduce-scatter.26.cloned.1.call-start = ((), (), s32[]{:S(2)}) async-start(), calls=%async_computation.22 | async-start | bytes 1572864 | tf_op jit(solution)/shard_map/reduce_scatter | solution.py:82
  972.0 5.2 copy-start.6
  972.0 142.6 %all-reduce.9.cloned.1.call-start = ((), (), s32[]{:S(2)}) async-start(), calls=%async_computation.23 | async-start | bytes 12582912 | tf_op jit(solution)/shard_map/psum | solution.py:294
  972.3 4.9 copy-start.34
  977.3 2.7 copy-start.7
  977.3 4.0 copy-start.10
  977.3 4.0 copy-start.11
  983.4 3.4 copy-start.12
  983.6 15.4 %copy-start.28 = (f32[256]{0:T(256)S(1)}, f32[256]{0:T(256)}, u32[]{:S(2)}) copy-start(f32[256]{0:T(256)} %param.20) | copy-start | bytes 3076
  986.6 37.1 %copy-start.21 = (f32[512,256]{1,0:T(8,128)S(1)}, f32[512,256]{1,0:T(8,128)}, u32[]{:S(2)}) copy-start(f32[512,256]{1,0:T(8,128)} %get-tuple-element.156) | copy-start | bytes 1572868
  1114.6 3.2 copy-start.25
  1114.6 4.0 copy-start.18
  1117.8 2.1 copy-start.17
  1118.6 2.6 copy-start.1
  (3 other events, 2.3 us)
Sparse Core Ops, SparseCore 0:
  35.6 108.9 reduce-scatter.9
  147.7 46.7 all-gather.5
  201.2 28.4 all-gather.7
  232.5 19.8 reduce-scatter.11
  254.7 143.6 reduce-scatter.17
  400.8 145.1 reduce-scatter.13
  549.8 81.4 all-gather.11
  633.6 79.2 all-gather.9
  715.8 18.8 reduce-scatter.19
  737.3 20.3 reduce-scatter.15
  770.7 43.8 reduce-scatter.21
  824.7 76.0 reduce-scatter.23
  904.1 63.9 all-gather.13
  972.2 18.4 reduce-scatter.25
  994.3 120.2 all-reduce.8
where the time goes:
time: 1130 us
  waiting for transfers between devices  909 us (80%)
  blocking collectives  104 us (9%)
  matrix products  53.8 us (5%)
  other arithmetic  30.3 us (3%)
  local copies, waits for them, and re-layouts  15.1 us (1%)
  between operations  14.3 us (1%)
    reduce_scatter x4, waiting for transfers between devices, across_rows(): lax.psum_scatter(partial_term(jnp.int32(0), row_count * lax.axis_size('ro...  422 us
    all_gather x4, waiting for transfers between devices, across_cols(): gathered = lax.all_gather(operand, 'row', axis=0, tiled=True)  250 us
    psum x1, waiting for transfers between devices, on_device(): lax.psum((weight_terms[0], weight_terms[1], weight_terms[2], weight_terms...  88.7 us
    reduce_scatter x1, waiting for transfers between devices, on_device(): lax.psum_scatter(jnp.stack([key_grad.reshape(-1, col_width), value_grad.r...  73.4 us
    all_gather x1, waiting for transfers between devices, on_device(): lax.all_gather(jnp.stack([keys_here, values_here], axis=1), 'row', axis=0...  44.8 us
    psum x4, blocking collectives, width_sums(): lax.psum((jnp.sum(first_term, axis=1), jnp.sum(second_term, axis=1)), 'row')  44.6 us
    all_gather x4, blocking collectives, across_rows(): gathered = lax.all_gather(operand, 'col', axis=0, tiled=True)  33.2 us
    reduce_scatter x4, waiting for transfers between devices, across_cols(): lax.psum_scatter(partial_term(jnp.int32(0), row_count * lax.axis_size('co...  29.8 us
  transfers between devices with their start and end apart: 15, of which 14 were waited for; matrix products, arithmetic and copies ran while one was open for 4% of the time, Pallas kernels for 0%

commit v1 on v0

--- a/solution.py
+++ b/solution.py
@@ -1,3 +1,4 @@
+import functools
 import math
 import jax
 import jax.numpy as jnp
@@ -7,6 +8,27 @@
 HD = 128
 EPS = 1e-05
 MASKED = -1e30
+
+
+def pair_the_modes(local_values, group_axis, on_dim):
+    amount_of = lax.axis_size(group_axis)
+    history = [(idx, (idx + 1) % amount_of) for idx in range(amount_of)]
+
+    def reach_cycles(big):
+        if len(big) == amount_of:
+            return big
+        tile_out = lax.ppermute(big[0], group_axis, history)
+        r_now = reach_cycles([tile_out, *big])
+        return r_now
+
+    now = reach_cycles([local_values])
+    main = jnp.concatenate(now, on_dim)
+    v1 = lax.axis_index(group_axis)
+    h_now = jnp.roll(main, (v1 + 1) * local_values.shape[on_dim], axis=on_dim)
+    return h_now
+
+
+_number_skins = functools.partial(pair_the_modes, group_axis="row", on_dim=0)
 
 
 def gelu_value(values):
@@ -72,7 +94,7 @@
 
 
 def across_cols(operand, weight_block, flipped):
-    gathered = lax.all_gather(operand, "row", axis=0, tiled=True)
+    gathered = _number_skins(operand)
     row_count = gathered.shape[0] // lax.axis_size("col")
 
     def partial_term(row_start, row_num):

time: 1130 us -> 1120 us (level)
  waiting for transfers between devices: 909 us -> 844 us
  other arithmetic: 30.3 us -> 63.4 us
  local copies, waits for them, and re-layouts: 15.1 us -> 28.6 us
    all_gather x4 -> x0, waiting for transfers between devices: 250 us -> none  [across_cols(): gathered = lax.all_gather(operand, 'row', axis=0, tiled=True)]
    ppermute x0 -> x12, waiting for transfers between devices: none -> 199 us  [reach_cycles(): tile_out = lax.ppermute(big[0], group_axis, history)]
    reduce_sum x1, other arithmetic: 3.02 us -> 23.6 us  [on_device(): jnp.sum(pre_all.astype(jnp.float32), axis=0)]
    reduce_scatter x4, waiting for transfers between devices: 29.8 us -> 14.6 us  [across_cols(): lax.psum_scatter(partial_term(jnp.int32(0), row_count * lax.axis_size('co...]
    concatenate x0 -> x1, other arithmetic: none -> 13.5 us  [pair_the_modes(): h_now = jnp.roll(main, (v1 + 1) * local_values.shape[on_dim], axis=on_dim)]
    unnamed x77 -> x101, local copies, waits for them, and re-layouts: 10.9 us -> 24.4 us
  transfers between devices with their start and end apart: 15 -> 23, of which waited for: 14 -> 21; matrix products, arithmetic and copies ran while one was open for 4% -> 7% of each run, Pallas kernels for 0% -> 0%
where the time goes in v1:
time: 1120 us; the launch traced here: 1110 us
  waiting for transfers between devices  844 us (75%)
  blocking collectives  105 us (9%)
  other arithmetic  63.4 us (6%)
  matrix products  45 us (4%)
  local copies, waits for them, and re-layouts  28.6 us (3%)
  between operations  14.7 us (1%)
    reduce_scatter x4, waiting for transfers between devices, across_rows(): lax.psum_scatter(partial_term(jnp.int32(0), row_count * lax.axis_size('ro...  421 us
    ppermute x12, waiting for transfers between devices, reach_cycles(): tile_out = lax.ppermute(big[0], group_axis, history)  199 us
    psum x1, waiting for transfers between devices, on_device(): lax.psum((weight_terms[0], weight_terms[1], weight_terms[2], weight_terms...  91 us
    reduce_scatter x1, waiting for transfers between devices, on_device(): lax.psum_scatter(jnp.stack([key_grad.reshape(-1, col_width), value_grad.r...  73.2 us
    all_gather x1, waiting for transfers between devices, on_device(): lax.all_gather(jnp.stack([keys_here, values_here], axis=1), 'row', axis=0...  45.8 us
    psum x4, blocking collectives, width_sums(): lax.psum((jnp.sum(first_term, axis=1), jnp.sum(second_term, axis=1)), 'row')  45.2 us
    all_gather x4, blocking collectives, across_rows(): gathered = lax.all_gather(operand, 'col', axis=0, tiled=True)  35 us
    unnamed x101, local copies, waits for them, and re-layouts  24.4 us
  transfers between devices with their start and end apart: 23, of which 21 were waited for; matrix products, arithmetic and copies ran while one was open for 7% of the time, Pallas kernels for 0%

profile of v1, /device:TPU:0, one launch (start us, length us, event | category | flops | bytes accessed | tf_op | source)
XLA Modules:
  0.0 1107.7 jit_solution(11871256982260891722)
XLA Ops:
  8.5 13.5 %all-reduce.4 = (f32[512]{0:T(512)S(1)}, f32[512]{0:T(512)S(1)}) all-reduce(f32[512]{0:T(512)S(1)} %get-tuple-element.135, f32[512]{0:T(512)S(1)} %get-tuple-element.134), channel_id=1, replica_groups=mesh['dp'=4,'row'=4,'col'=2] {'row'}, use_global_device_ids=true, to_apply=%region_3.4 | all-reduce | flops 1024 | bytes 8192 | tf_op jit(solution)/shard_map/psum | solution.py:45
  23.1 7.0 all_gather.15
  31.8 3.7 fusion.73
  36.2 108.4 %reduce-scatter.10.cloned.1.call-done = f32[256,1536]{1,0:T(8,128)} async-done(((f32[1024,1536]{1,0:T(8,128)}), f32[256,1536]{1,0:T(8,128)}) %reduce-scatter.10.cloned.1.call-update) | async-done | bytes 1572880 | tf_op jit(solution)/shard_map/reduce_scatter | solution.py:86
  148.8 45.8 %all-gather.2.cloned.1.call-done = bf16[1024,2,512]{0,2,1:T(8,128)(2,1)} async-done(((bf16[256,2,512]{0,2,1:T(8,128)(2,1)}), bf16[1024,2,512]{0,2,1:T(8,128)(2,1)}) %all-gather.2.cloned.1.call-update) | async-done | bytes 2097168 | tf_op jit(solution)/shard_map/all_gather | solution.py:247
  201.5 9.0 collective-permute-done
  210.5 8.2 collective-permute-done.1
  218.7 8.2 collective-permute-done.2
  228.5 2.4 fusion.34
  231.0 12.2 %all_gather.18 = bf16[1024,256]{1,0:T(8,128)(2,1)S(1)} all-gather(bf16[512,256]{1,0:T(8,128)(2,1)S(1)} %copy-done.30), channel_id=1, replica_groups=mesh['dp'=4,'row'=4,'col'=2] {'col'}, dimensions={0}, use_global_device_ids=true | all-gather | bytes 786432 | tf_op jit(solution)/shard_map/all_gather | solution.py:79
  244.0 4.5 fusion.76
  248.6 3.3 reduce-scatter.12.cloned.1.call-done
  253.1 11.6 %all-reduce.3 = (f32[512]{0:T(512)S(1)}, f32[512]{0:T(512)S(1)}) all-reduce(f32[512]{0:T(512)S(1)} %get-tuple-element.133, f32[512]{0:T(512)S(1)} %get-tuple-element.132), channel_id=1, replica_groups=mesh['dp'=4,'row'=4,'col'=2] {'row'}, use_global_device_ids=true, to_apply=%region_13.14 | all-reduce | flops 1024 | bytes 8192 | tf_op jit(solution)/shard_map/psum | solution.py:45
  264.9 7.0 all_gather.17
  272.8 4.5 fusion.74
  277.8 120.7 %reduce-scatter.18.cloned.1.call-done = f32[256,2048]{1,0:T(8,128)} async-done(((f32[1024,2048]{1,0:T(8,128)}), f32[256,2048]{1,0:T(8,128)}) %reduce-scatter.18.cloned.1.call-update) | async-done | bytes 2097168 | tf_op jit(solution)/shard_map/reduce_scatter | solution.py:86
  398.5 147.5 %reduce-scatter.14.cloned.1.call-done = f32[256,2048]{1,0:T(8,128)} async-done(((f32[1024,2048]{1,0:T(8,128)}), f32[256,2048]{1,0:T(8,128)}) %reduce-scatter.14.cloned.1.call-update) | async-done | bytes 2097168 | tf_op jit(solution)/shard_map/reduce_scatter | solution.py:86
  545.9 2.7 fusion.25
  549.9 2.5 collective-permute-start.3
  552.4 24.2 %collective-permute-done.6 = bf16[256,2048]{1,0:T(8,128)(2,1)S(1)} collective-permute-done((bf16[256,2048]{1,0:T(8,128)(2,1)S(1)}, bf16[256,2048]{1,0:T(8,128)(2,1)S(1)}, u32[]{:S(2)}, u32[]{:S(2)}) %collective-permute-start.6) | collective-permute-done | bytes 1048608 | tf_op jit(solution)/shard_map/ppermute | solution.py:20
  576.6 22.5 %collective-permute-done.3 = bf16[256,2048]{1,0:T(8,128)(2,1)S(1)} collective-permute-done((bf16[256,2048]{1,0:T(8,128)(2,1)S(1)}, bf16[256,2048]{1,0:T(8,128)(2,1)S(1)}, u32[]{:S(2)}, u32[]{:S(2)}) %collective-permute-start.3) | collective-permute-done | bytes 1048608 | tf_op jit(solution)/shard_map/ppermute | solution.py:20
  599.1 22.5 %collective-permute-done.7 = bf16[256,2048]{1,0:T(8,128)(2,1)S(1)} collective-permute-done((bf16[256,2048]{1,0:T(8,128)(2,1)S(1)}, bf16[256,2048]{1,0:T(8,128)(2,1)S(1)}, u32[]{:S(2)}, u32[]{:S(2)}) %collective-permute-start.7) | collective-permute-done | bytes 1048608 | tf_op jit(solution)/shard_map/ppermute | solution.py:20
  621.5 22.6 %collective-permute-done.4 = bf16[256,2048]{1,0:T(8,128)(2,1)} collective-permute-done((bf16[256,2048]{1,0:T(8,128)(2,1)S(1)}, bf16[256,2048]{1,0:T(8,128)(2,1)}, u32[]{:S(2)}, u32[]{:S(2)}) %collective-permute-start.4) | collective-permute-done | bytes 1048608 | tf_op jit(solution)/shard_map/ppermute | solution.py:20
  644.1 22.4 %collective-permute-done.8 = bf16[256,2048]{1,0:T(8,128)(2,1)S(1)} collective-permute-done((bf16[256,2048]{1,0:T(8,128)(2,1)S(1)}, bf16[256,2048]{1,0:T(8,128)(2,1)S(1)}, u32[]{:S(2)}, u32[]{:S(2)}) %collective-permute-start.8) | collective-permute-done | bytes 1048608 | tf_op jit(solution)/shard_map/ppermute | solution.py:20
  666.5 23.6 %convert_reduce_fusion = (f32[2048]{0:T(1024)S(1)}, bf16[1024,2048]{1,0:T(8,128)(2,1)S(1)}) fusion(s32[]{:T(128)S(6)} %select_n.105, bf16[256,2048]{1,0:T(8,128)(2,1)S(1)} %get-tuple-element.161, bf16[256,2048]{1,0:T(8,128)(2,1)S(1)} %collective-permute-done.6, bf16[256,2048]{1,0:T(8,128)(2,1)S(1)} %collective-permute-done.7, ...), kind=kLoop, calls=%fused_computation.16 | loop fusion | flops 37746688 | bytes 8396804 | tf_op jit(solution)/shard_map/reduce_sum | solution.py:303
  694.7 13.5 %fusion.10 = bf16[1024,2048]{1,0:T(8,128)(2,1)S(1)} fusion(s32[]{:T(128)S(6)} %select_n.105, bf16[256,2048]{1,0:T(8,128)(2,1)} %collective-permute-done.5, bf16[256,2048]{1,0:T(8,128)(2,1)} %collective-permute-done.4, bf16[256,2048]{1,0:T(8,128)(2,1)} %copy-done.29, bf16[256,2048]{1,0:T(8,128)(2,1)S(1)} %get-tuple-element.162), kind=kLoop, calls=%fused_computation.28 | loop fusion | flops 33554432 | bytes 8388612 | tf_op jit(solution)/shard_map/jit(_roll_dynamic)/concatenate | solution.py:27
  715.2 11.7 %all-reduce.2 = (f32[512]{0:T(512)S(1)}, f32[512]{0:T(512)S(1)}) all-reduce(f32[512]{0:T(512)S(1)} %get-tuple-element.125, f32[512]{0:T(512)S(1)} %get-tuple-element.129), channel_id=1, replica_groups=mesh['dp'=4,'row'=4,'col'=2] {'row'}, use_global_device_ids=true, to_apply=%region_21.23 | all-reduce | flops 1024 | bytes 8192 | tf_op jit(solution)/shard_map/psum | solution.py:45
  726.9 10.0 reduce-scatter.16.cloned.1.call-done
  736.9 2.4 fusion.66
  739.4 8.7 all_gather.19
  750.0 44.0 %reduce-scatter.22.cloned.1.call-done = f32[256,512]{1,0:T(8,128)} async-done(((f32[1024,512]{1,0:T(8,128)}), f32[256,512]{1,0:T(8,128)}) %reduce-scatter.22.cloned.1.call-update) | async-done | bytes 524304 | tf_op jit(solution)/shard_map/reduce_scatter | solution.py:86
  795.2 3.2 fusion.26
  801.5 2.4 pad_maximum_fusion
  804.1 2.8 fusion.30
  806.9 73.2 %reduce-scatter.24.cloned.1.call-done = f32[256,2,512]{0,2,1:T(8,128)} async-done(((f32[1024,2,512]{0,2,1:T(8,128)}), f32[256,2,512]{0,2,1:T(8,128)}) %reduce-scatter.24.cloned.1.call-update) | async-done | bytes 1048592 | tf_op jit(solution)/shard_map/reduce_scatter | solution.py:276
  883.9 19.6 %collective-permute-done.9 = bf16[256,1536]{0,1:T(8,128)(2,1)S(1)} collective-permute-done((bf16[256,1536]{0,1:T(8,128)(2,1)S(1)}, bf16[256,1536]{0,1:T(8,128)(2,1)S(1)}, u32[]{:S(2)}, u32[]{:S(2)}) %collective-permute-start.9) | collective-permute-done | bytes 786464 | tf_op jit(solution)/shard_map/ppermute | solution.py:20
  903.5 20.3 %collective-permute-done.10 = bf16[256,1536]{0,1:T(8,128)(2,1)S(1)} collective-permute-done((bf16[256,1536]{0,1:T(8,128)(2,1)S(1)}, bf16[256,1536]{0,1:T(8,128)(2,1)S(1)}, u32[]{:S(2)}, u32[]{:S(2)}) %collective-permute-start.10) | collective-permute-done | bytes 786464 | tf_op jit(solution)/shard_map/ppermute | solution.py:20
  923.8 19.3 %collective-permute-done.11 = bf16[256,1536]{0,1:T(8,128)(2,1)S(1)} collective-permute-done((bf16[256,1536]{0,1:T(8,128)(2,1)S(1)}, bf16[256,1536]{0,1:T(8,128)(2,1)S(1)}, u32[]{:S(2)}, u32[]{:S(2)}) %collective-permute-start.11) | collective-permute-done | bytes 786464 | tf_op jit(solution)/shard_map/ppermute | solution.py:20
  944.1 2.7 copy-done.21
  948.8 4.9 fusion.79
  953.8 2.7 fusion.80
  960.8 2.4 convert_reduce_fusion.1
  963.2 10.7 all-reduce.5
  975.4 14.3 %all-reduce = (f32[256]{0:T(256)}, f32[256]{0:T(256)}, f32[256]{0:T(256)}, f32[256]{0:T(256)}) all-reduce(f32[256]{0:T(256)S(1)} %get-tuple-element.126, f32[256]{0:T(256)S(1)} %get-tuple-element.131, f32[256]{0:T(256)S(1)} %get-tuple-element.124, f32[256]{0:T(256)S(1)} %get-tuple-element.130), channel_id=1, replica_groups=mesh['dp'=4,'row'=4,'col'=2] {'dp','col'}, use_global_device_ids=true, to_apply=%region_31.33 | all-reduce | flops 1024 | bytes 8192 | tf_op jit(solution)/shard_map/psum | solution.py:335
  989.7 8.5 all-reduce.1
  1000.4 91.0 %all-reduce.9.cloned.1.call-done = (f32[256,3,512]{0,2,1:T(8,128)}, f32[512,256]{1,0:T(8,128)}, f32[256,2048]{1,0:T(8,128)}, f32[2048,256]{1,0:T(8,128)}) async-done(((f32[256,3,512]{0,2,1:T(8,128)}, f32[512,256]{1,0:T(8,128)}, f32[256,2048]{1,0:T(8,128)}, f32[2048,256]{1,0:T(8,128)}), (f32[256,3,512]{0,2,1:T(8,128)}, f32[512,256]{1,0:T(8,128)}, f32[256,2048]{1,0:T(8,128)}, ...) | async-done | bytes 6291472 | tf_op jit(solution)/shard_map/psum | solution.py:316
  1091.4 3.2 copy.55
  1096.5 3.1 copy.80
  (186 shorter events, 58.0 us)
Async XLA Ops:
  7.2 265.6 %copy-start = (bf16[256,2048]{1,0:T(8,128)(2,1)S(1)}, bf16[256,2048]{1,0:T(8,128)(2,1)}, u32[]{:S(2)}) copy-start(bf16[256,2048]{1,0:T(8,128)(2,1)} %param.30) | copy-start | bytes 3145732
  7.2 137.4 %reduce-scatter.10.cloned.1.call-start = ((), (), s32[]{:S(2)}) async-start(), calls=%async_computation.9 | async-start | bytes 7864320 | tf_op jit(solution)/shard_map/reduce_scatter | solution.py:86
  30.2 5.3 copy-start.13
  31.8 3.7 copy-start.15
  35.5 112.2 %copy-start.32 = (s32[1024]{0:T(1024)S(1)}, s32[1024]{0:T(1024)}, u32[]{:S(2)}) copy-start(s32[1024]{0:T(1024)} %param.21) | copy-start | bytes 12292
  35.5 112.4 %copy-start.40 = (s32[13]{0:T(128)S(1)}, s32[13]{0:T(128)}, u32[]{:S(2)}) copy-start(s32[13]{0:T(128)} %param.20) | copy-start | bytes 160
  35.5 159.0 %all-gather.2.cloned.1.call-start = ((), (), s32[]{:S(2)}) async-start(), calls=%async_computation.10 | async-start | bytes 2621440 | tf_op jit(solution)/shard_map/all_gather | solution.py:247
  146.7 52.3 %copy-start.24 = (f32[256,1,512]{0,2,1:T(8,128)}, f32[256,1,512]{0,2,1:T(8,128)S(1)}, u32[]{:S(2)}) copy-start(f32[256,1,512]{0,2,1:T(8,128)S(1)} %get-tuple-element.165) | copy-start | bytes 1572868
  147.6 104.2 %reduce-scatter.12.cloned.1.call-start = ((), (), s32[]{:S(2)}) async-start(), calls=%async_computation.11 | async-start | bytes 1572864 | tf_op jit(solution)/shard_map/reduce_scatter | solution.py:104
  196.3 3.8 copy-start.11
  201.2 29.7 %copy-start.30 = (bf16[512,256]{1,0:T(8,128)(2,1)S(1)}, bf16[512,256]{1,0:T(8,128)(2,1)}, u32[]{:S(2)}) copy-start(bf16[512,256]{1,0:T(8,128)(2,1)} %param.19) | copy-start | bytes 786436
  201.2 9.2 collective-permute-start
  210.5 8.2 collective-permute-start.1
  218.7 8.2 collective-permute-start.2
  218.7 25.3 %copy-start.27 = (bf16[2048,256]{1,0:T(8,128)(2,1)S(1)}, bf16[2048,256]{1,0:T(8,128)(2,1)}, u32[]{:S(2)}) copy-start(bf16[2048,256]{1,0:T(8,128)(2,1)} %param.32) | copy-start | bytes 3145732
  230.9 167.6 %reduce-scatter.18.cloned.1.call-start = ((), (), s32[]{:S(2)}) async-start(), calls=%async_computation.14 | async-start | bytes 10485760 | tf_op jit(solution)/shard_map/reduce_scatter | solution.py:86
  248.5 16.2 %copy-start.33 = (f32[256]{0:T(256)S(1)}, f32[256]{0:T(256)}, u32[]{:S(2)}) copy-start(f32[256]{0:T(256)} %param.28) | copy-start | bytes 3076
  248.5 16.2 %copy-start.37 = (f32[256]{0:T(256)S(1)}, f32[256]{0:T(256)}, u32[]{:S(2)}) copy-start(f32[256]{0:T(256)} %param.29) | copy-start | bytes 3076
  248.5 297.4 %reduce-scatter.14.cloned.1.call-start = ((), (), s32[]{:S(2)}) async-start(), calls=%async_computation.12 | async-start | bytes 10485760 | tf_op jit(solution)/shard_map/reduce_scatter | solution.py:86
  277.2 268.7 %copy-start.35 = (f32[2048]{0:T(1024)S(1)}, f32[2048]{0:T(1024)}, u32[]{:S(2)}) copy-start(f32[2048]{0:T(1024)} %param.31) | copy-start | bytes 24580
  277.3 436.5 %reduce-scatter.20.cloned.1.call-start = ((), (), s32[]{:S(2)}) async-start(), calls=%async_computation.15 | async-start | bytes 1572864 | tf_op jit(solution)/shard_map/reduce_scatter | solution.py:104
  548.7 27.9 %collective-permute-start.6 = (bf16[256,2048]{1,0:T(8,128)(2,1)S(1)}, bf16[256,2048]{1,0:T(8,128)(2,1)S(1)}, u32[]{:S(2)}, u32[]{:S(2)}) collective-permute-start(bf16[256,2048]{1,0:T(8,128)(2,1)S(1)} %get-tuple-element.161), channel_id=1, source_target_pairs={{0,2},{2,4},{4,6},{6,0},{1,3},{3,5},{5,7},{7,1},{8,10},{10,12},{12... | collective-permute-start | bytes 3145736 | tf_op jit(solution)/shard_map/ppermute | solution.py:20
  549.9 49.2 %collective-permute-start.3 = (bf16[256,2048]{1,0:T(8,128)(2,1)S(1)}, bf16[256,2048]{1,0:T(8,128)(2,1)S(1)}, u32[]{:S(2)}, u32[]{:S(2)}) collective-permute-start(bf16[256,2048]{1,0:T(8,128)(2,1)S(1)} %get-tuple-element.162), channel_id=1, source_target_pairs={{0,2},{2,4},{4,6},{6,0},{1,3},{3,5},{5,7},{7,1},{8,10},{10,12},{12... | collective-permute-start | bytes 3145736 | tf_op jit(solution)/shard_map/ppermute | solution.py:20
  576.6 44.9 %collective-permute-start.7 = (bf16[256,2048]{1,0:T(8,128)(2,1)S(1)}, bf16[256,2048]{1,0:T(8,128)(2,1)S(1)}, u32[]{:S(2)}, u32[]{:S(2)}) collective-permute-start(bf16[256,2048]{1,0:T(8,128)(2,1)S(1)} %collective-permute-done.6), channel_id=1, source_target_pairs={{0,2},{2,4},{4,6},{6,0},{1,3},{3,5},{5,7},{7,1},{8,10},{10,12},{12... | collective-permute-start | bytes 3145736 | tf_op jit(solution)/shard_map/ppermute | solution.py:20
  599.1 45.1 %copy-start.29 = (bf16[256,2048]{1,0:T(8,128)(2,1)}, bf16[256,2048]{1,0:T(8,128)(2,1)S(1)}, u32[]{:S(2)}) copy-start(bf16[256,2048]{1,0:T(8,128)(2,1)S(1)} %collective-permute-done.3) | copy-start | bytes 3145732
  599.1 45.0 %collective-permute-start.4 = (bf16[256,2048]{1,0:T(8,128)(2,1)S(1)}, bf16[256,2048]{1,0:T(8,128)(2,1)}, u32[]{:S(2)}, u32[]{:S(2)}) collective-permute-start(bf16[256,2048]{1,0:T(8,128)(2,1)S(1)} %collective-permute-done.3), channel_id=1, source_target_pairs={{0,2},{2,4},{4,6},{6,0},{1,3},{3,5},{5,7},{7,1},{8,10},{10,12},{12... | collective-permute-start | bytes 3145736 | tf_op jit(solution)/shard_map/ppermute | solution.py:20
  621.5 44.9 %collective-permute-start.8 = (bf16[256,2048]{1,0:T(8,128)(2,1)S(1)}, bf16[256,2048]{1,0:T(8,128)(2,1)S(1)}, u32[]{:S(2)}, u32[]{:S(2)}) collective-permute-start(bf16[256,2048]{1,0:T(8,128)(2,1)S(1)} %collective-permute-done.7), channel_id=1, source_target_pairs={{0,2},{2,4},{4,6},{6,0},{1,3},{3,5},{5,7},{7,1},{8,10},{10,12},{12... | collective-permute-start | bytes 3145736 | tf_op jit(solution)/shard_map/ppermute | solution.py:20
  644.1 50.6 %collective-permute-start.5 = (bf16[256,2048]{1,0:T(8,128)(2,1)}, bf16[256,2048]{1,0:T(8,128)(2,1)}, u32[]{:S(2)}, u32[]{:S(2)}) collective-permute-start(bf16[256,2048]{1,0:T(8,128)(2,1)} %collective-permute-done.4), channel_id=1, source_target_pairs={{0,2},{2,4},{4,6},{6,0},{1,3},{3,5},{5,7},{7,1},{8,10},{10,12},{12... | collective-permute-start | bytes 3145736 | tf_op jit(solution)/shard_map/ppermute | solution.py:20
  694.4 15.9 %copy-start.28 = (bf16[2048,256]{1,0:T(8,128)(2,1)S(1)}, bf16[2048,256]{1,0:T(8,128)(2,1)}, u32[]{:S(2)}) copy-start(bf16[2048,256]{1,0:T(8,128)(2,1)} %param.32) | copy-start | bytes 3145732
  694.4 42.5 %reduce-scatter.16.cloned.1.call-start = ((), (), s32[]{:S(2)}) async-start(), calls=%async_computation.13 | async-start | bytes 1572864 | tf_op jit(solution)/shard_map/reduce_scatter | solution.py:104
  710.3 26.7 %copy-start.38 = (f32[256]{0:T(256)S(1)}, f32[256]{0:T(256)}, u32[]{:S(2)}) copy-start(f32[256]{0:T(256)} %param.33) | copy-start | bytes 3076
  712.5 35.6 %copy-start.31 = (bf16[512,256]{1,0:T(8,128)(2,1)S(1)}, bf16[512,256]{1,0:T(8,128)(2,1)}, u32[]{:S(2)}) copy-start(bf16[512,256]{1,0:T(8,128)(2,1)} %param.26) | copy-start | bytes 786436
  712.5 81.4 %reduce-scatter.22.cloned.1.call-start = ((), (), s32[]{:S(2)}) async-start(), calls=%async_computation.16 | async-start | bytes 2621440 | tf_op jit(solution)/shard_map/reduce_scatter | solution.py:86
  749.9 48.5 %copy-start.12 = (bf16[1024,1,512]{0,2,1:T(8,128)(2,1)S(1)}, bf16[1024,1,512]{0,2,1:T(8,128)(2,1)}, u32[]{:S(2)}) copy-start(bf16[1024,1,512]{0,2,1:T(8,128)(2,1)} %copy-done.11) | copy-start | bytes 3145732
  749.9 130.1 %reduce-scatter.24.cloned.1.call-start = ((), (), s32[]{:S(2)}) async-start(), calls=%async_computation.17 | async-start | bytes 5242880 | tf_op jit(solution)/shard_map/reduce_scatter | solution.py:276
  803.8 170.1 %reduce-scatter.26.cloned.1.call-start = ((), (), s32[]{:S(2)}) async-start(), calls=%async_computation.18 | async-start | bytes 1572864 | tf_op jit(solution)/shard_map/reduce_scatter | solution.py:104
  882.4 21.2 %collective-permute-start.9 = (bf16[256,1536]{0,1:T(8,128)(2,1)S(1)}, bf16[256,1536]{0,1:T(8,128)(2,1)S(1)}, u32[]{:S(2)}, u32[]{:S(2)}) collective-permute-start(bf16[256,1536]{0,1:T(8,128)(2,1)S(1)} %bitcast.54), channel_id=1, source_target_pairs={{0,2},{2,4},{4,6},{6,0},{1,3},{3,5},{5,7},{7,1},{8,10},{10,12},{12... | collective-permute-start | bytes 2359304 | tf_op jit(solution)/shard_map/ppermute | solution.py:20
  903.5 20.3 %collective-permute-start.10 = (bf16[256,1536]{0,1:T(8,128)(2,1)S(1)}, bf16[256,1536]{0,1:T(8,128)(2,1)S(1)}, u32[]{:S(2)}, u32[]{:S(2)}) collective-permute-start(bf16[256,1536]{0,1:T(8,128)(2,1)S(1)} %collective-permute-done.9), channel_id=1, source_target_pairs={{0,2},{2,4},{4,6},{6,0},{1,3},{3,5},{5,7},{7,1},{8,10},{10,12},{12... | collective-permute-start | bytes 2359304 | tf_op jit(solution)/shard_map/ppermute | solution.py:20
  923.8 19.3 %collective-permute-start.11 = (bf16[256,1536]{0,1:T(8,128)(2,1)S(1)}, bf16[256,1536]{0,1:T(8,128)(2,1)S(1)}, u32[]{:S(2)}, u32[]{:S(2)}) collective-permute-start(bf16[256,1536]{0,1:T(8,128)(2,1)S(1)} %collective-permute-done.10), channel_id=1, source_target_pairs={{0,2},{2,4},{4,6},{6,0},{1,3},{3,5},{5,7},{7,1},{8,10},{10,12},{12... | collective-permute-start | bytes 2359304 | tf_op jit(solution)/shard_map/ppermute | solution.py:20
  948.7 5.0 copy-start.6
  948.8 142.6 %all-reduce.9.cloned.1.call-start = ((), (), s32[]{:S(2)}) async-start(), calls=%async_computation.19 | async-start | bytes 12582912 | tf_op jit(solution)/shard_map/psum | solution.py:316
  948.8 4.9 copy-start.9
  953.8 4.0 copy-start.14
  953.8 4.5 copy-start.22
  960.4 13.5 %copy-start.34 = (f32[256]{0:T(256)S(1)}, f32[256]{0:T(256)}, u32[]{:S(2)}) copy-start(f32[256]{0:T(256)} %param.22) | copy-start | bytes 3076
  960.4 37.7 %copy-start.26 = (f32[512,256]{1,0:T(8,128)S(1)}, f32[512,256]{1,0:T(8,128)}, u32[]{:S(2)}) copy-start(f32[512,256]{1,0:T(8,128)} %get-tuple-element.159) | copy-start | bytes 1572868
  1091.4 8.3 copy-start.23
  1094.5 6.4 copy-start.1
  (16 other events, 33.0 us)
Sparse Core Ops, SparseCore 0:
  35.6 108.9 reduce-scatter.9
  147.8 46.7 all-gather.1
  231.0 20.7 reduce-scatter.11
  254.2 144.2 reduce-scatter.17
  400.8 145.0 reduce-scatter.13
  694.5 19.2 reduce-scatter.19
  716.6 20.2 reduce-scatter.15
  750.0 43.8 reduce-scatter.21
  804.0 76.0 reduce-scatter.23
  948.9 18.4 reduce-scatter.25
  971.1 120.2 all-reduce.8
